TPU v7x, 128 devices: a whole 4x4x4 slice. The times are simulated.
128 devices in a mesh: pipe: 2 (over x_hi), tensor: 4 (over z), dp: 16 (over x_lo, y, core).
Axes of the slice: x: 4 (x_hi: 2, x_lo: 2; x = x_hi * 2 + x_lo), y: 4, z: 4, core: 2. Of those that a mesh axis runs over, the one named last changes fastest.
Arguments:
- tokens: bfloat16 [8192, 1024], P('dp', 'tensor'), may hold values from -6 to 6
- lengths: int32 [64, 4], P('dp'), may hold values from 1 to 85, 128 in all within a row
- ln_gain: bfloat16 [2, 2, 1024], P('pipe'), may hold values from 0.099609375 to 1.8984375
- ln_bias: bfloat16 [2, 2, 1024], P('pipe'), may hold values from -3 to 3
- joined_weight: bfloat16 [2, 1024, 3, 1024], P('pipe', None, None, 'tensor'), may hold values from -0.1875 to 0.1875
- joined_bias: bfloat16 [2, 3, 1024], P('pipe', None, 'tensor'), may hold values from -3 to 3
- dense_weight: bfloat16 [2, 1024, 1024], P('pipe', 'tensor'), may hold values from -0.5 to 0.5
- up_weight: bfloat16 [2, 1024, 4096], P('pipe', None, 'tensor'), may hold values from -0.1875 to 0.1875
- up_bias: bfloat16 [2, 4096], P('pipe', 'tensor'), may hold values from -3 to 3
- down_weight: bfloat16 [2, 4096, 1024], P('pipe', 'tensor'), may hold values from -0.09375 to 0.09375
- output_bias: bfloat16 [2, 2, 1024], P('pipe'), may hold values from -3 to 3
- cotangent: bfloat16 [8192, 1024], P('dp', 'tensor'), may hold values from -6 to 6
Outputs:
- section_out: bfloat16 [2, 8192, 1024], P('pipe', 'dp', 'tensor')
- input_grad: bfloat16 [2, 8192, 1024], P('pipe', 'dp', 'tensor')
- grad_ln_gain: float32 [2, 2, 1024], P('pipe')
- grad_ln_bias: float32 [2, 2, 1024], P('pipe')
- grad_joined: float32 [2, 1024, 3, 1024], P('pipe', None, None, 'tensor')
- grad_joined_bias: float32 [2, 3, 1024], P('pipe', None, 'tensor')
- grad_dense: float32 [2, 1024, 1024], P('pipe', 'tensor')
- grad_up: float32 [2, 1024, 4096], P('pipe', None, 'tensor')
- grad_up_bias: float32 [2, 4096], P('pipe', 'tensor')
- grad_down: float32 [2, 4096, 1024], P('pipe', 'tensor')
- grad_output_bias: float32 [2, 2, 1024], P('pipe')
Inputs may be any that keep to these rules, and one draw needn't show every extreme that they name: Row b gives, in order, the lengths of the 4 sequences that fill block b (tokens b * 128 to (b + 1) * 128 - 1); every row sums to 128.
All inputs are finite; a program needn't handle non-finite values.
Results may differ from a plain program's by a relative error of at most 0.035.
Values may be sent and summed in bfloat16 or wider, within the bound.
No kernel may reach another device: no remote copies, remote signals or barrier semaphores. Data moves between devices by JAX's collectives and lax.ppermute only.
A program may use at most 192 MiB of HBM per device.

v0:
```python
import jax
import jax.numpy as jnp
from jax import lax
from jax.sharding import PartitionSpec as P

HD = 64
ROT = 16
MB = 128
NMB = 4
EPSILON = 1e-05
MASKED = -1e30


def passed_along(x, axis, by):
    peers = lax.axis_size(axis)
    pairs = [(i, i + by) for i in range(peers) if 0 <= i + by < peers]
    return lax.ppermute(x, axis, pairs)


def as_sent(x):
    return jax.tree.map(lambda a: a.astype(jnp.bfloat16) if a.dtype == jnp.float32 else a, x)


def positions(lengths, block_rows):
    seq_count = lengths.shape[1]
    counter = jnp.arange(seq_count, dtype=jnp.int32)
    lower_tri = (counter[:, None] >= counter[None, :]).astype(jnp.int32)
    seg_ends = jnp.sum(lengths[:, None, :] * lower_tri[None, :, :], axis=2)
    starts = seg_ends - lengths
    row_index = jnp.arange(block_rows, dtype=jnp.int32)
    segment = jnp.sum((row_index[None, :, None] >= seg_ends[:, None, :]).astype(jnp.int32), axis=2)
    member = (segment[:, :, None] == counter[None, None, :]).astype(jnp.int32)
    place = row_index[None, :] - jnp.sum(member * starts[:, None, :], axis=2)
    return (segment, place)


def rotary(place):
    half_rot = ROT // 2
    inv_freq = jnp.power(10000.0, -2.0 * jnp.arange(half_rot, dtype=jnp.float32) / ROT)
    angles = place.astype(jnp.float32)[..., None] * inv_freq
    return (jnp.cos(angles), jnp.sin(angles))


def rotate(heads_in, cosv, sinv):
    half_rot = ROT // 2
    first_half = heads_in[..., :half_rot]
    second_half = heads_in[..., half_rot:ROT]
    cos_rows = cosv[:, None, :]
    sin_rows = sinv[:, None, :]
    return jnp.concatenate(
        [
            first_half * cos_rows - second_half * sin_rows,
            second_half * cos_rows + first_half * sin_rows,
            heads_in[..., ROT:],
        ],
        axis=-1,
    )


def rotate_back(heads_in, cosv, sinv):
    half_rot = ROT // 2
    first_half = heads_in[..., :half_rot]
    second_half = heads_in[..., half_rot:ROT]
    cos_rows = cosv[:, None, :]
    sin_rows = sinv[:, None, :]
    return jnp.concatenate(
        [
            first_half * cos_rows + second_half * sin_rows,
            second_half * cos_rows - first_half * sin_rows,
            heads_in[..., ROT:],
        ],
        axis=-1,
    )


def exact_gelu(values):
    return jax.nn.gelu(values, approximate=False)


def allowed_keys(segment):
    row_index = jnp.arange(segment.shape[0], dtype=jnp.int32)
    return (segment[:, None] == segment[None, :]) & (row_index[None, :] <= row_index[:, None])


def contract_rows(left, right):
    return lax.dot_general(
        left, right, (((0,), (0,)), ((), ())), preferred_element_type=jnp.float32
    )


def contract_cols(left, right):
    return lax.dot_general(
        left, right, (((1,), (1,)), ((), ())), preferred_element_type=jnp.float32
    )


def per_device(
    tokens,
    lengths,
    ln_gain,
    ln_bias,
    joined_weight,
    joined_bias,
    dense_weight,
    up_weight,
    up_bias,
    down_weight,
    output_bias,
    cotangent,
):
    leading = lax.axis_index("pipe") == 0
    model_width = joined_weight.shape[1]
    local_width = joined_weight.shape[3]
    local_heads = local_width // HD
    hidden_local = up_weight.shape[2]
    quarter = tokens.shape[1]
    score_scale = HD ** (-0.5)
    ln_gains = ln_gain[0].astype(jnp.float32)
    ln_shifts = ln_bias[0].astype(jnp.float32)
    joined_mat = joined_weight[0].reshape(model_width, 3 * local_width)
    joined_add = joined_bias[0].astype(jnp.float32).reshape(3 * local_width)
    dense_mat = dense_weight[0]
    up_mat = up_weight[0]
    up_add = up_bias[0].astype(jnp.float32)
    down_mat = down_weight[0]
    bias_sum = output_bias[0, 0].astype(jnp.float32) + output_bias[0, 1].astype(jnp.float32)
    gathered_rows = lax.all_gather(
        jnp.concatenate([tokens, cotangent], axis=0), "tensor", axis=1, tiled=True
    )
    input_rows = gathered_rows[: tokens.shape[0]]
    output_grads = gathered_rows[tokens.shape[0] :]
    segment_all, place_all = positions(lengths, MB)
    cos_all, sin_all = rotary(place_all)

    def pick(early_val, late_val):
        return jax.tree.map(
            lambda upper_val, lower_val: jnp.where(leading, upper_val, lower_val),
            early_val,
            late_val,
        )

    received = jnp.zeros((MB, model_width), jnp.bfloat16)
    tick_outputs = []
    tick_stored = []
    for section_tick in range(NMB + 1):
        early_block = min(section_tick, NMB - 1)
        late_block = max(section_tick - 1, 0)
        block_rows = jnp.where(
            leading, input_rows[early_block * MB : (early_block + 1) * MB], received
        )
        segment, cosv, sinv = pick(
            (segment_all[early_block], cos_all[early_block], sin_all[early_block]),
            (segment_all[late_block], cos_all[late_block], sin_all[late_block]),
        )
        inputs = block_rows.astype(jnp.float32)
        row_mean = jnp.mean(inputs, axis=1, keepdims=True)
        centred = inputs - row_mean
        forward_inv_scale = lax.rsqrt(jnp.mean(centred * centred, axis=1, keepdims=True) + EPSILON)
        forward_normed = centred * forward_inv_scale
        forward_h_attn = (forward_normed * ln_gains[0] + ln_shifts[0]).astype(jnp.bfloat16)
        forward_h_mlp = (forward_normed * ln_gains[1] + ln_shifts[1]).astype(jnp.bfloat16)
        joined_proj = (
            jnp.dot(forward_h_attn, joined_mat, preferred_element_type=jnp.float32) + joined_add
        )
        forward_block_len = block_rows.shape[0]
        forward_queries = rotate(
            joined_proj[:, :local_width].reshape(forward_block_len, local_heads, HD), cosv, sinv
        ).astype(jnp.bfloat16)
        forward_keys_rot = rotate(
            joined_proj[:, local_width : 2 * local_width].reshape(
                forward_block_len, local_heads, HD
            ),
            cosv,
            sinv,
        ).astype(jnp.bfloat16)
        forward_values = (
            joined_proj[:, 2 * local_width :]
            .reshape(forward_block_len, local_heads, HD)
            .astype(jnp.bfloat16)
        )
        forward_scores = (
            jnp.einsum(
                "qhd,khd->hqk",
                forward_queries,
                forward_keys_rot,
                preferred_element_type=jnp.float32,
            )
            * score_scale
        )
        forward_scores = jnp.where(allowed_keys(segment)[None], forward_scores, MASKED)
        row_top = jnp.max(forward_scores, axis=2, keepdims=True)
        exponent = jnp.exp(forward_scores - row_top)
        row_total = jnp.sum(exponent, axis=2, keepdims=True)
        forward_log_total = row_top + jnp.log(row_total)
        weights_low = (exponent / row_total).astype(jnp.bfloat16)
        forward_context = jnp.einsum(
            "hqk,khd->qhd", weights_low, forward_values, preferred_element_type=jnp.float32
        )
        forward_context = forward_context.reshape(forward_block_len, local_width).astype(
            jnp.bfloat16
        )
        forward_up_proj = (
            jnp.dot(forward_h_mlp, up_mat, preferred_element_type=jnp.float32) + up_add
        )
        forward_activated = exact_gelu(forward_up_proj).astype(jnp.bfloat16)
        partial_value = jnp.dot(forward_context, dense_mat, preferred_element_type=jnp.float32)
        partial_value = partial_value + jnp.dot(
            forward_activated, down_mat, preferred_element_type=jnp.float32
        )
        branches = lax.psum(partial_value.astype(jnp.bfloat16), "tensor").astype(jnp.float32)
        result = inputs + branches + bias_sum
        forward_stored = (
            forward_normed,
            forward_inv_scale,
            forward_h_attn,
            forward_h_mlp,
            forward_queries,
            forward_keys_rot,
            forward_values,
            forward_log_total,
            forward_context,
            forward_up_proj,
            forward_activated,
        )
        result, stored = (result, forward_stored)
        result_low = result.astype(jnp.bfloat16)
        tick_outputs.append(result_low)
        tick_stored.append((stored, segment, cosv, sinv))
        if section_tick < NMB:
            received = passed_along(result_low, "pipe", 1)
    column_start = lax.axis_index("tensor") * quarter
    section_rows = jnp.concatenate(
        [jnp.where(leading, tick_outputs[block], tick_outputs[block + 1]) for block in range(NMB)],
        axis=0,
    )
    section_out = lax.dynamic_slice_in_dim(section_rows, column_start, quarter, 1)[None]
    returned = jnp.zeros((MB, model_width), jnp.bfloat16)
    tick_grads = []
    totals = None
    for section_tick in range(NMB + 1):
        own_block = min(section_tick, NMB - 1)
        late_tick = max(section_tick - 1, 0)
        upper_tick = min(section_tick + 1, NMB)
        from_output = output_grads[own_block * MB : (own_block + 1) * MB]
        if section_tick == NMB:
            from_output = jnp.zeros_like(from_output)
        grad_rows = jnp.where(leading, returned, from_output)
        stored, segment, cosv, sinv = pick(tick_stored[late_tick], tick_stored[upper_tick])
        (
            normed,
            inv_scale,
            h_attn,
            h_mlp,
            queries,
            keys_rot,
            values,
            log_total,
            context,
            up_proj,
            activated,
        ) = stored
        block_len = grad_rows.shape[0]
        grad_wide = grad_rows.astype(jnp.float32)
        column_sum = jnp.sum(grad_wide, axis=0)
        backward_grad_dense = contract_rows(context, grad_rows)
        backward_grad_down = contract_rows(activated, grad_rows)
        d_context = contract_cols(grad_rows, dense_mat).astype(jnp.bfloat16)
        d_act = contract_cols(grad_rows, down_mat)
        unused, slope_back = jax.vjp(exact_gelu, up_proj)
        d_up = slope_back(d_act)[0].astype(jnp.bfloat16)
        grad_up_add = jnp.sum(d_up.astype(jnp.float32), axis=0)
        backward_grad_up = contract_rows(h_mlp, d_up)
        d_hmlp = contract_cols(d_up, up_mat)
        scores = (
            jnp.einsum("qhd,khd->hqk", queries, keys_rot, preferred_element_type=jnp.float32)
            * score_scale
        )
        scores = jnp.where(allowed_keys(segment)[None], scores, MASKED)
        weights_soft = jnp.exp(scores - log_total)
        d_context3 = d_context.reshape(block_len, local_heads, HD)
        d_values = jnp.einsum(
            "hqk,qhd->khd",
            weights_soft.astype(jnp.bfloat16),
            d_context3,
            preferred_element_type=jnp.float32,
        ).astype(jnp.bfloat16)
        d_weights = jnp.einsum(
            "qhd,khd->hqk", d_context3, values, preferred_element_type=jnp.float32
        )
        row_delta = jnp.sum(weights_soft * d_weights, axis=2, keepdims=True)
        d_scores = (weights_soft * (d_weights - row_delta)).astype(jnp.bfloat16)
        d_queries = (
            jnp.einsum("hqk,khd->qhd", d_scores, keys_rot, preferred_element_type=jnp.float32)
            * score_scale
        )
        d_keys = (
            jnp.einsum("hqk,qhd->khd", d_scores, queries, preferred_element_type=jnp.float32)
            * score_scale
        )
        d_queries = (
            rotate_back(d_queries, cosv, sinv).reshape(block_len, local_width).astype(jnp.bfloat16)
        )
        d_keys = (
            rotate_back(d_keys, cosv, sinv).reshape(block_len, local_width).astype(jnp.bfloat16)
        )
        d_joined = jnp.concatenate(
            [d_queries, d_keys, d_values.reshape(block_len, local_width)], axis=1
        )
        grad_joined_add = jnp.sum(d_joined.astype(jnp.float32), axis=0)
        backward_grad_joined = contract_rows(d_joined, h_attn)
        d_hattn = contract_cols(d_joined, joined_mat)
        d_hattn, d_hmlp = (
            lax.psum(d_hattn.astype(jnp.bfloat16), "tensor").astype(jnp.float32),
            lax.psum(d_hmlp.astype(jnp.bfloat16), "tensor").astype(jnp.float32),
        )
        grad_gains = jnp.concatenate(
            [jnp.sum(d_hattn * normed, axis=0), jnp.sum(d_hmlp * normed, axis=0)]
        )
        grad_shifts = jnp.concatenate([jnp.sum(d_hattn, axis=0), jnp.sum(d_hmlp, axis=0)])
        d_norm = d_hattn * ln_gains[0] + d_hmlp * ln_gains[1]
        grad_input = grad_wide + inv_scale * (
            d_norm
            - jnp.mean(d_norm, axis=1, keepdims=True)
            - normed * jnp.mean(d_norm * normed, axis=1, keepdims=True)
        )
        small_terms = jnp.concatenate(
            [grad_gains, grad_shifts, column_sum, column_sum, grad_joined_add, grad_up_add]
        )
        terms = (
            backward_grad_joined[None],
            backward_grad_dense[None],
            backward_grad_up[None],
            backward_grad_down[None],
            small_terms[None],
        )
        grad_input, terms = (grad_input, terms)
        grad_low = grad_input.astype(jnp.bfloat16)
        tick_grads.append(grad_low)
        if totals is None:
            totals = terms
        else:
            totals = jax.tree.map(lambda older, newer: older + newer, totals, terms)
        if section_tick < NMB:
            returned = passed_along(grad_low, "pipe", -1)
    small_rows = totals[4][0]
    small_pad = -small_rows.shape[0] % model_width
    small_rows = jnp.pad(small_rows, (0, small_pad)).reshape(-1, model_width)
    pieces = (totals[0][0], totals[1][0], totals[2][0], totals[3][0], small_rows)
    slab = jnp.concatenate([piece.astype(jnp.bfloat16) for piece in pieces], axis=0)
    slab = lax.psum(slab, "dp").astype(jnp.float32)
    summed = []
    offset = 0
    for piece in pieces:
        summed.append(slab[offset : offset + piece.shape[0]])
        offset = offset + piece.shape[0]
    grad_rows_all = jnp.concatenate(
        [jnp.where(leading, tick_grads[block + 1], tick_grads[block]) for block in range(NMB)],
        axis=0,
    )
    input_grad = lax.dynamic_slice_in_dim(grad_rows_all, column_start, quarter, 1)[None]
    grad_joined = summed[0].T.reshape(1, model_width, 3, local_width)
    grad_dense = summed[1][None]
    grad_up = summed[2][None]
    grad_down = summed[3][None]
    small_sum = summed[4].reshape(-1)
    offset = 0
    grad_ln_gain = small_sum[offset : offset + 2 * model_width].reshape(1, 2, model_width)
    offset = offset + 2 * model_width
    grad_ln_bias = small_sum[offset : offset + 2 * model_width].reshape(1, 2, model_width)
    offset = offset + 2 * model_width
    grad_output_bias = small_sum[offset : offset + 2 * model_width].reshape(1, 2, model_width)
    offset = offset + 2 * model_width
    grad_joined_bias = small_sum[offset : offset + 3 * local_width].reshape(1, 3, local_width)
    offset = offset + 3 * local_width
    grad_up_bias = small_sum[offset : offset + hidden_local].reshape(1, hidden_local)
    return (
        section_out,
        input_grad,
        grad_ln_gain,
        grad_ln_bias,
        grad_joined,
        grad_joined_bias,
        grad_dense,
        grad_up,
        grad_up_bias,
        grad_down,
        grad_output_bias,
    )


def solution(mesh):
    placed = (
        P("dp", "tensor"),
        P("dp", None),
        P("pipe", None, None),
        P("pipe", None, None),
        P("pipe", None, None, "tensor"),
        P("pipe", None, "tensor"),
        P("pipe", "tensor", None),
        P("pipe", None, "tensor"),
        P("pipe", "tensor"),
        P("pipe", "tensor", None),
        P("pipe", None, None),
        P("dp", "tensor"),
    )
    return jax.shard_map(
        per_device,
        mesh=mesh,
        in_specs=placed,
        out_specs=(
            P("pipe", "dp", "tensor"),
            P("pipe", "dp", "tensor"),
            P("pipe", None, None),
            P("pipe", None, None),
            P("pipe", None, None, "tensor"),
            P("pipe", None, "tensor"),
            P("pipe", "tensor", None),
            P("pipe", None, "tensor"),
            P("pipe", "tensor"),
            P("pipe", "tensor", None),
            P("pipe", None, None),
        ),
        check_vma=False,
    )
```

profile of v0, /device:TPU:25, one launch (start us, length us, event | category | flops | bytes accessed | tf_op | source)
XLA Modules:
  0.0 722.0 jit_solution(4068381418110488269)
XLA Ops:
  24.7 21.6 %all-gather.2.cloned.1.call-done = bf16[1024,1024]{1,0:T(8,128)(2,1)} async-done(((bf16[1024,256]{1,0:T(8,128)(2,1)}), bf16[1024,1024]{1,0:T(8,128)(2,1)}) %all-gather.2.cloned.1.call-update) | async-done | bytes 2097168 | tf_op jit(solution)/shard_map/all_gather | solution.py:127
  58.8 41.0 %all-reduce.14.cloned.1.call-done = bf16[128,1024]{1,0:T(8,128)(2,1)} async-done(((bf16[128,1024]{1,0:T(8,128)(2,1)}), bf16[128,1024]{1,0:T(8,128)(2,1)}) %all-reduce.14.cloned.1.call-update) | async-done | bytes 262160 | tf_op jit(solution)/shard_map/psum | solution.py:210
  100.9 5.1 collective-permute-start
  128.4 3.6 convert_reduce_fusion.24
  134.9 3.9 fusion.386
  142.9 5.4 fusion.377
  148.3 34.1 %all-reduce.26.cloned.1.call-done = (bf16[128,1024]{1,0:T(8,128)(2,1)}, bf16[128,1024]{1,0:T(8,128)(2,1)}, bf16[128,1024]{1,0:T(8,128)(2,1)}) async-done(((bf16[128,1024]{1,0:T(8,128)(2,1)}, bf16[128,1024]{1,0:T(8,128)(2,1)}, bf16[128,1024]{1,0:T(8,128)(2,1)}), (bf16[128,1024]{1,0:T(8,128)(2,1)}, bf16[128,1024]{1,0:T(8,128)(2,1)}, bf16[128,1024]{1,0:T(8,128)(2,1)})) %all-reduce.26.cloned.1.call-update) | async-done | bytes 786448 | tf_op jit(solution)/shard_map/psum | solution.py:210
  187.9 5.7 collective-permute-start.1
  231.0 4.0 fusion.384
  239.3 4.5 fusion.375
  243.8 35.5 %all-reduce.24.cloned.1.call-done = (bf16[128,1024]{1,0:T(8,128)(2,1)}, bf16[128,1024]{1,0:T(8,128)(2,1)}, bf16[128,1024]{1,0:T(8,128)(2,1)}) async-done(((bf16[128,1024]{1,0:T(8,128)(2,1)}, bf16[128,1024]{1,0:T(8,128)(2,1)}, bf16[128,1024]{1,0:T(8,128)(2,1)}), (bf16[128,1024]{1,0:T(8,128)(2,1)}, bf16[128,1024]{1,0:T(8,128)(2,1)}, bf16[128,1024]{1,0:T(8,128)(2,1)})) %all-reduce.24.cloned.1.call-update) | async-done | bytes 786448 | tf_op jit(solution)/shard_map/psum | solution.py:210
  285.6 5.7 collective-permute-start.2
  336.3 4.4 fusion.373
  340.7 39.9 %all-reduce.22.cloned.1.call-done = (bf16[128,1024]{1,0:T(8,128)(2,1)}, bf16[128,1024]{1,0:T(8,128)(2,1)}, bf16[128,1024]{1,0:T(8,128)(2,1)}) async-done(((bf16[128,1024]{1,0:T(8,128)(2,1)}, bf16[128,1024]{1,0:T(8,128)(2,1)}, bf16[128,1024]{1,0:T(8,128)(2,1)}), (bf16[128,1024]{1,0:T(8,128)(2,1)}, bf16[128,1024]{1,0:T(8,128)(2,1)}, bf16[128,1024]{1,0:T(8,128)(2,1)})) %all-reduce.22.cloned.1.call-update) | async-done | bytes 786448 | tf_op jit(solution)/shard_map/psum | solution.py:210
  386.2 6.0 collective-permute-start.3
  424.8 4.0 fusion.380
  428.9 4.4 fusion.371
  442.2 40.8 %all-reduce.20.cloned.1.call-done = (bf16[128,1024]{1,0:T(8,128)(2,1)}, bf16[128,1024]{1,0:T(8,128)(2,1)}) async-done(((bf16[128,1024]{1,0:T(8,128)(2,1)}, bf16[128,1024]{1,0:T(8,128)(2,1)}), (bf16[128,1024]{1,0:T(8,128)(2,1)}, bf16[128,1024]{1,0:T(8,128)(2,1)})) %all-reduce.20.cloned.1.call-update) | async-done | bytes 524304 | tf_op jit(solution)/shard_map/psum | solution.py:314
  507.9 6.9 fusion.42
  523.8 6.8 fusion
  530.6 23.6 %all-reduce.18.cloned.1.call-done = (bf16[128,1024]{1,0:T(8,128)(2,1)}, bf16[128,1024]{1,0:T(8,128)(2,1)}, bf16[128,1024]{1,0:T(8,128)(2,1)}) async-done(((bf16[128,1024]{1,0:T(8,128)(2,1)}, bf16[128,1024]{1,0:T(8,128)(2,1)}, bf16[128,1024]{1,0:T(8,128)(2,1)}), (bf16[128,1024]{1,0:T(8,128)(2,1)}, bf16[128,1024]{1,0:T(8,128)(2,1)}, bf16[128,1024]{1,0:T(8,128)(2,1)})) %all-reduce.18.cloned.1.call-update) | async-done | bytes 786448 | tf_op jit(solution)/shard_map/psum | solution.py:210
  560.9 135.7 %all-reduce.16.cloned.1.call-done = bf16[3080,1024]{1,0:T(8,128)(2,1)} async-done(((bf16[3080,1024]{1,0:T(8,128)(2,1)}), bf16[3080,1024]{1,0:T(8,128)(2,1)}) %all-reduce.16.cloned.1.call-update) | async-done | bytes 6307856 | tf_op jit(solution)/shard_map/psum | solution.py:350
  696.6 4.3 convert_element_type.684
  702.6 4.2 slice_bitcast_fusion
  (916 shorter events, 252.5 us)
Async XLA Ops:
  7.2 48.7 %copy-start = (bf16[1,1024,1024]{2,1,0:T(8,128)(2,1)S(1)}, bf16[1,1024,1024]{2,1,0:T(8,128)(2,1)}, u32[]{:S(2)}) copy-start(bf16[1,1024,1024]{2,1,0:T(8,128)(2,1)} %param.21) | copy-start | bytes 6291460
  7.2 39.1 %all-gather.2.cloned.1.call-start = ((), (), s32[]{:S(2)}) async-start(), calls=%async_computation | async-start | bytes 2621440 | tf_op jit(solution)/shard_map/all_gather | solution.py:127
  9.3 90.5 %all-reduce.14.cloned.1.call-start = ((), (), s32[]{:S(2)}) async-start(), calls=%async_computation.1 | async-start | bytes 524288 | tf_op jit(solution)/shard_map/psum | solution.py:210
  55.9 50.2 %copy-start.281 = (s32[128]{0:T(128)S(1)}, s32[128]{0:T(128)}, u32[]{:S(2)}) copy-start(s32[128]{0:T(128)} %get-tuple-element.106) | copy-start | bytes 1540
  55.9 50.2 %copy-start.282 = (s32[128]{0:T(128)S(1)}, s32[128]{0:T(128)}, u32[]{:S(2)}) copy-start(s32[128]{0:T(128)} %get-tuple-element.246) | copy-start | bytes 1540
  58.1 124.3 %all-reduce.26.cloned.1.call-start = ((), (), s32[]{:S(2)}) async-start(), calls=%async_computation.7 | async-start | bytes 1572864 | tf_op jit(solution)/shard_map/psum | solution.py:210
  58.2 48.6 %copy-start.90 = (f32[1,1,1024]{2,1,0:T(1,128)}, f32[1,1,1024]{2,1,0:T(1,128)S(1)}, u32[]{:S(2)}) copy-start(f32[1,1,1024]{2,1,0:T(1,128)S(1)} %convert_add_fusion.10) | copy-start | bytes 12292
  100.9 7.9 %collective-permute-start = (bf16[128,1024]{1,0:T(8,128)(2,1)S(1)}, bf16[128,1024]{1,0:T(8,128)(2,1)S(1)}, u32[]{:S(2)}, u32[]{:S(2)}) collective-permute-start(bf16[128,1024]{1,0:T(8,128)(2,1)S(1)} %fusion.193), channel_id=1, source_target_pairs={{0,64},{1,65},{2,66},{3,67},{4,68},{5,69},{6,70},{7,71},{8,72},{9,... | collective-permute-start | bytes 786440 | tf_op jit(solution)/shard_map/ppermute | solution.py:17
  134.8 144.6 %all-reduce.24.cloned.1.call-start = ((), (), s32[]{:S(2)}) async-start(), calls=%async_computation.6 | async-start | bytes 1572864 | tf_op jit(solution)/shard_map/psum | solution.py:210
  185.7 8.6 %collective-permute-start.4 = (bf16[128,1024]{1,0:T(8,128)(2,1)S(1)}, bf16[128,1024]{1,0:T(8,128)(2,1)S(1)}, u32[]{:S(2)}, u32[]{:S(2)}) collective-permute-start(bf16[128,1024]{1,0:T(8,128)(2,1)S(1)} %fusion.187), channel_id=1, source_target_pairs={{64,0},{65,1},{66,2},{67,3},{68,4},{69,5},{70,6},{71,7},{72,8},{73... | collective-permute-start | bytes 786440 | tf_op jit(solution)/shard_map/ppermute | solution.py:17
  187.9 8.8 %collective-permute-start.1 = (bf16[128,1024]{1,0:T(8,128)(2,1)S(1)}, bf16[128,1024]{1,0:T(8,128)(2,1)S(1)}, u32[]{:S(2)}, u32[]{:S(2)}) collective-permute-start(bf16[128,1024]{1,0:T(8,128)(2,1)S(1)} %get-tuple-element.133), channel_id=1, source_target_pairs={{0,64},{1,65},{2,66},{3,67},{4,68},{5,69},{6,70},{7,71},{8,72},{9,... | collective-permute-start | bytes 786440 | tf_op jit(solution)/shard_map/ppermute | solution.py:17
  198.6 82.6 %copy-start.21 = (bf16[128,1024]{1,0:T(8,128)(2,1)}, bf16[128,1024]{1,0:T(8,128)(2,1)S(1)}, u32[]{:S(2)}) copy-start(bf16[128,1024]{1,0:T(8,128)(2,1)S(1)} %get-tuple-element.91) | copy-start | bytes 786436
  230.9 149.6 %all-reduce.22.cloned.1.call-start = ((), (), s32[]{:S(2)}) async-start(), calls=%async_computation.5 | async-start | bytes 1572864 | tf_op jit(solution)/shard_map/psum | solution.py:210
  283.2 9.5 %collective-permute-start.5 = (bf16[128,1024]{1,0:T(8,128)(2,1)S(1)}, bf16[128,1024]{1,0:T(8,128)(2,1)S(1)}, u32[]{:S(2)}, u32[]{:S(2)}) collective-permute-start(bf16[128,1024]{1,0:T(8,128)(2,1)S(1)} %get-tuple-element.101), channel_id=1, source_target_pairs={{64,0},{65,1},{66,2},{67,3},{68,4},{69,5},{70,6},{71,7},{72,8},{73... | collective-permute-start | bytes 786440 | tf_op jit(solution)/shard_map/ppermute | solution.py:17
  285.6 8.8 %collective-permute-start.2 = (bf16[128,1024]{1,0:T(8,128)(2,1)S(1)}, bf16[128,1024]{1,0:T(8,128)(2,1)S(1)}, u32[]{:S(2)}, u32[]{:S(2)}) collective-permute-start(bf16[128,1024]{1,0:T(8,128)(2,1)S(1)} %get-tuple-element.128), channel_id=1, source_target_pairs={{0,64},{1,65},{2,66},{3,67},{4,68},{5,69},{6,70},{7,71},{8,72},{9,... | collective-permute-start | bytes 786440 | tf_op jit(solution)/shard_map/ppermute | solution.py:17
  332.1 150.8 %all-reduce.20.cloned.1.call-start = ((), (), s32[]{:S(2)}) async-start(), calls=%async_computation.4 | async-start | bytes 1048576 | tf_op jit(solution)/shard_map/psum | solution.py:314
  336.3 44.3 %copy-start.118 = (f32[128]{0:T(128)S(1)}, f32[128]{0:T(128)}, u32[]{:S(2)}) copy-start(f32[128]{0:T(128)} %copy-done.116) | copy-start | bytes 1540
  336.3 45.9 %copy-start.93 = (f32[1,1,1024]{2,1,0:T(1,128)S(1)}, f32[1,1,1024]{2,1,0:T(1,128)}, u32[]{:S(2)}) copy-start(f32[1,1,1024]{2,1,0:T(1,128)} %copy-done.90) | copy-start | bytes 12292
  336.3 45.9 %copy-start.277 = (f32[128]{0:T(128)S(1)}, f32[128]{0:T(128)}, u32[]{:S(2)}) copy-start(f32[128]{0:T(128)} %get-tuple-element.263) | copy-start | bytes 1540
  384.9 8.6 %collective-permute-start.6 = (bf16[128,1024]{1,0:T(8,128)(2,1)S(1)}, bf16[128,1024]{1,0:T(8,128)(2,1)S(1)}, u32[]{:S(2)}, u32[]{:S(2)}) collective-permute-start(bf16[128,1024]{1,0:T(8,128)(2,1)S(1)} %get-tuple-element.99), channel_id=1, source_target_pairs={{64,0},{65,1},{66,2},{67,3},{68,4},{69,5},{70,6},{71,7},{72,8},{73... | collective-permute-start | bytes 786440 | tf_op jit(solution)/shard_map/ppermute | solution.py:17
  386.2 8.8 %collective-permute-start.3 = (bf16[128,1024]{1,0:T(8,128)(2,1)S(1)}, bf16[128,1024]{1,0:T(8,128)(2,1)S(1)}, u32[]{:S(2)}, u32[]{:S(2)}) collective-permute-start(bf16[128,1024]{1,0:T(8,128)(2,1)S(1)} %get-tuple-element.160), channel_id=1, source_target_pairs={{0,64},{1,65},{2,66},{3,67},{4,68},{5,69},{6,70},{7,71},{8,72},{9,... | collective-permute-start | bytes 786440 | tf_op jit(solution)/shard_map/ppermute | solution.py:17
  436.4 117.8 %all-reduce.18.cloned.1.call-start = ((), (), s32[]{:S(2)}) async-start(), calls=%async_computation.3 | async-start | bytes 1572864 | tf_op jit(solution)/shard_map/psum | solution.py:210
  486.9 8.8 %collective-permute-start.7 = (bf16[128,1024]{1,0:T(8,128)(2,1)S(1)}, bf16[128,1024]{1,0:T(8,128)(2,1)S(1)}, u32[]{:S(2)}, u32[]{:S(2)}) collective-permute-start(bf16[128,1024]{1,0:T(8,128)(2,1)S(1)} %get-tuple-element.97), channel_id=1, source_target_pairs={{64,0},{65,1},{66,2},{67,3},{68,4},{69,5},{70,6},{71,7},{72,8},{73... | collective-permute-start | bytes 786440 | tf_op jit(solution)/shard_map/ppermute | solution.py:17
  507.8 188.7 %all-reduce.16.cloned.1.call-start = ((), (), s32[]{:S(2)}) async-start(), calls=%async_computation.2 | async-start | bytes 12615680 | tf_op jit(solution)/shard_map/psum | solution.py:350
  (282 other events, 2324.1 us)
Sparse Core Ops, SparseCore 0:
  10.3 35.9 all-gather.1
  58.2 41.5 all-reduce.13
  134.9 47.4 all-reduce.25
  231.0 48.2 all-reduce.23
  332.3 48.2 all-reduce.21
  436.5 46.3 all-reduce.19
  507.9 46.2 all-reduce.17
  557.5 139.0 all-reduce.15
where the time goes:
time: 729 us; the launch traced here: 722 us
  waiting for transfers between devices  381 us (52%)
  matrix products  156 us (21%)
  other arithmetic  69 us (9%)
  local copies, waits for them, and re-layouts  68.4 us (9%)
  starting transfers between devices  28.3 us (4%)
  between operations  18.4 us (3%)
    psum x5, waiting for transfers between devices, per_device(): lax.psum(partial_value.astype(jnp.bfloat16), 'tensor').astype(jnp.float32)  174 us
    psum x1, waiting for transfers between devices, per_device(): slab = lax.psum(slab, 'dp').astype(jnp.float32)  136 us
    dot_general x20, matrix products, contract_rows(): lax.dot_general(left, right, (((0,), (0,)), ((), ())), preferred_element_...  68.6 us
    psum x1, waiting for transfers between devices, per_device(): lax.psum(d_hmlp.astype(jnp.bfloat16), 'tensor').astype(jnp.float32)  40.8 us
    dot_general x20, matrix products, contract_cols(): lax.dot_general(left, right, (((1,), (1,)), ((), ())), preferred_element_...  32.1 us
    ppermute x8, starting transfers between devices, passed_along(): return lax.ppermute(x, axis, pairs)  27.9 us
    all_gather x1, waiting for transfers between devices, per_device(): lax.all_gather(jnp.concatenate([tokens, cotangent], axis=0), 'tensor', ax...  21.6 us
    unnamed x619, local copies, waits for them, and re-layouts  20.5 us
  transfers between devices with their start and end apart: 16, of which 15 were waited for; matrix products, arithmetic and copies ran while one was open for 12% of the time, Pallas kernels for 0%

commit v1 on v0

--- a/solution.py
+++ b/solution.py
@@ -2,6 +2,7 @@
 import jax.numpy as jnp
 from jax import lax
 from jax.sharding import PartitionSpec as P
+from jax.lax import all_gather
 
 HD = 64
 ROT = 16
@@ -309,9 +310,14 @@
         grad_joined_add = jnp.sum(d_joined.astype(jnp.float32), axis=0)
         backward_grad_joined = contract_rows(d_joined, h_attn)
         d_hattn = contract_cols(d_joined, joined_mat)
+
+        def keep_up_the_set(row_data, device_axis):
+            clean = all_gather(row_data, axis_name=device_axis)
+            return jnp.sum(clean, axis=0)
+
         d_hattn, d_hmlp = (
             lax.psum(d_hattn.astype(jnp.bfloat16), "tensor").astype(jnp.float32),
-            lax.psum(d_hmlp.astype(jnp.bfloat16), "tensor").astype(jnp.float32),
+            keep_up_the_set(d_hmlp.astype(jnp.bfloat16), "tensor").astype(jnp.float32),
         )
         grad_gains = jnp.concatenate(
             [jnp.sum(d_hattn * normed, axis=0), jnp.sum(d_hmlp * normed, axis=0)]

time: 729 us -> 813 us (1.12)
  waiting for transfers between devices: 381 us -> 443 us
  other arithmetic: 69 us -> 81 us
    all_gather x0 -> x5, waiting for transfers between devices: none -> 51.1 us  [keep_up_the_set(): clean = all_gather(row_data, axis_name=device_axis)]
    ppermute x8, waiting for transfers between devices: 9.19 us -> 19.7 us  [passed_along(): return lax.ppermute(x, axis, pairs)]
    reduce_sum x0 -> x5, other arithmetic: none -> 9.43 us  [keep_up_the_set(): return jnp.sum(clean, axis=0)]
    unnamed x619 -> x631, local copies, waits for them, and re-layouts: 20.5 us -> 21.7 us
  transfers between devices with their start and end apart: 16 -> 21, of which waited for: 15 -> 18; matrix products, arithmetic and copies ran while one was open for 12% -> 19% of each run, Pallas kernels for 0% -> 0%
where the time goes in v1:
time: 813 us; the launch traced here: 803 us
  waiting for transfers between devices  443 us (54%)
  matrix products  159 us (20%)
  other arithmetic  81 us (10%)
  local copies, waits for them, and re-layouts  72.1 us (9%)
  starting transfers between devices  28.7 us (4%)
  between operations  18.1 us (2%)
    psum x5, waiting for transfers between devices, per_device(): lax.psum(partial_value.astype(jnp.bfloat16), 'tensor').astype(jnp.float32)  174 us
    psum x1, waiting for transfers between devices, per_device(): slab = lax.psum(slab, 'dp').astype(jnp.float32)  136 us
    dot_general x20, matrix products, contract_rows(): lax.dot_general(left, right, (((0,), (0,)), ((), ())), preferred_element_...  71.4 us
    all_gather x5, waiting for transfers between devices, keep_up_the_set(): clean = all_gather(row_data, axis_name=device_axis)  51.1 us
    psum x1, waiting for transfers between devices, per_device(): lax.psum(d_hattn.astype(jnp.bfloat16), 'tensor').astype(jnp.float32)  41.2 us
    dot_general x20, matrix products, contract_cols(): lax.dot_general(left, right, (((1,), (1,)), ((), ())), preferred_element_...  34.4 us
    ppermute x8, starting transfers between devices, passed_along(): return lax.ppermute(x, axis, pairs)  26.7 us
    unnamed x631, local copies, waits for them, and re-layouts  21.7 us
  transfers between devices with their start and end apart: 21, of which 18 were waited for; matrix products, arithmetic and copies ran while one was open for 19% of the time, Pallas kernels for 0%

profile of v1, /device:TPU:25, one launch (start us, length us, event | category | flops | bytes accessed | tf_op | source)
XLA Modules:
  0.0 802.5 jit_solution(4029072418604809444)
XLA Ops:
  25.4 21.1 %all-gather.12.cloned.1.call-done = bf16[1024,1024]{1,0:T(8,128)(2,1)} async-done(((bf16[1024,256]{1,0:T(8,128)(2,1)}), bf16[1024,1024]{1,0:T(8,128)(2,1)}) %all-gather.12.cloned.1.call-update) | async-done | bytes 2097168 | tf_op jit(solution)/shard_map/all_gather | solution.py:128
  59.0 40.7 %all-reduce.13.cloned.1.call-done = bf16[128,1024]{1,0:T(8,128)(2,1)} async-done(((bf16[128,1024]{1,0:T(8,128)(2,1)}), bf16[128,1024]{1,0:T(8,128)(2,1)}) %all-reduce.13.cloned.1.call-update) | async-done | bytes 262160 | tf_op jit(solution)/shard_map/psum | solution.py:211
  100.9 5.3 collective-permute-start
  136.9 5.5 fusion.377
  142.4 27.2 %all-reduce.25.cloned.1.call-done = (bf16[128,1024]{1,0:T(8,128)(2,1)}, bf16[128,1024]{1,0:T(8,128)(2,1)}) async-done(((bf16[128,1024]{1,0:T(8,128)(2,1)}, bf16[128,1024]{1,0:T(8,128)(2,1)}), (bf16[128,1024]{1,0:T(8,128)(2,1)}, bf16[128,1024]{1,0:T(8,128)(2,1)})) %all-reduce.25.cloned.1.call-update) | async-done | bytes 524304 | tf_op jit(solution)/shard_map/psum | solution.py:211
  171.4 5.3 collective-permute-start.1
  176.7 20.8 %all-gather.14.cloned.1.call-done = bf16[512,1024]{1,0:T(8,128)(2,1)} async-done(((bf16[128,1024]{1,0:T(8,128)(2,1)}), bf16[512,1024]{1,0:T(8,128)(2,1)}) %all-gather.14.cloned.1.call-update) | async-done | bytes 1048592 | tf_op jit(solution)/shard_map/all_gather | solution.py:315
  203.4 8.2 %collective-permute-done.4 = bf16[128,1024]{1,0:T(8,128)(2,1)S(1)} collective-permute-done((bf16[128,1024]{1,0:T(8,128)(2,1)S(1)}, bf16[128,1024]{1,0:T(8,128)(2,1)S(1)}, u32[]{:S(2)}, u32[]{:S(2)}) %collective-permute-start.4) | collective-permute-done | bytes 262176 | tf_op jit(solution)/shard_map/ppermute | solution.py:18
  254.0 4.5 fusion.375
  258.5 23.7 %all-reduce.23.cloned.1.call-done = (bf16[128,1024]{1,0:T(8,128)(2,1)}, bf16[128,1024]{1,0:T(8,128)(2,1)}) async-done(((bf16[128,1024]{1,0:T(8,128)(2,1)}, bf16[128,1024]{1,0:T(8,128)(2,1)}), (bf16[128,1024]{1,0:T(8,128)(2,1)}, bf16[128,1024]{1,0:T(8,128)(2,1)})) %all-reduce.23.cloned.1.call-update) | async-done | bytes 524304 | tf_op jit(solution)/shard_map/psum | solution.py:211
  284.2 5.2 collective-permute-start.2
  289.4 20.7 %all-gather.16.cloned.1.call-done = bf16[512,1024]{1,0:T(8,128)(2,1)} async-done(((bf16[128,1024]{1,0:T(8,128)(2,1)}), bf16[512,1024]{1,0:T(8,128)(2,1)}) %all-gather.16.cloned.1.call-update) | async-done | bytes 1048592 | tf_op jit(solution)/shard_map/all_gather | solution.py:315
  367.8 6.2 fusion.373
  385.9 43.0 %all-reduce.21.cloned.1.call-done = (bf16[128,1024]{1,0:T(8,128)(2,1)}, bf16[128,1024]{1,0:T(8,128)(2,1)}) async-done(((bf16[128,1024]{1,0:T(8,128)(2,1)}, bf16[128,1024]{1,0:T(8,128)(2,1)}), (bf16[128,1024]{1,0:T(8,128)(2,1)}, bf16[128,1024]{1,0:T(8,128)(2,1)})) %all-reduce.21.cloned.1.call-update) | async-done | bytes 524304 | tf_op jit(solution)/shard_map/psum | solution.py:211
  434.6 5.5 collective-permute-start.3
  487.4 4.4 fusion.371
  497.5 6.5 all-gather.20.cloned.1.call-done
  506.2 41.2 %all-reduce.15.cloned.1.call-done = bf16[128,1024]{1,0:T(8,128)(2,1)} async-done(((bf16[128,1024]{1,0:T(8,128)(2,1)}), bf16[128,1024]{1,0:T(8,128)(2,1)}) %all-reduce.15.cloned.1.call-update) | async-done | bytes 262160 | tf_op jit(solution)/shard_map/psum | solution.py:319
  554.1 5.9 collective-permute-done.7
  571.0 6.9 fusion.42
  586.9 6.9 fusion
  595.5 39.7 %all-reduce.19.cloned.1.call-done = (bf16[128,1024]{1,0:T(8,128)(2,1)}, bf16[128,1024]{1,0:T(8,128)(2,1)}) async-done(((bf16[128,1024]{1,0:T(8,128)(2,1)}, bf16[128,1024]{1,0:T(8,128)(2,1)}), (bf16[128,1024]{1,0:T(8,128)(2,1)}, bf16[128,1024]{1,0:T(8,128)(2,1)})) %all-reduce.19.cloned.1.call-update) | async-done | bytes 524304 | tf_op jit(solution)/shard_map/psum | solution.py:211
  641.8 135.6 %all-reduce.17.cloned.1.call-done = bf16[3080,1024]{1,0:T(8,128)(2,1)} async-done(((bf16[3080,1024]{1,0:T(8,128)(2,1)}), bf16[3080,1024]{1,0:T(8,128)(2,1)}) %all-reduce.17.cloned.1.call-update) | async-done | bytes 6307856 | tf_op jit(solution)/shard_map/psum | solution.py:356
  777.4 4.3 convert_element_type.694
  (948 shorter events, 290.0 us)
Async XLA Ops:
  7.2 39.3 %all-gather.12.cloned.1.call-start = ((), (), s32[]{:S(2)}) async-start(), calls=%async_computation | async-start | bytes 2621440 | tf_op jit(solution)/shard_map/all_gather | solution.py:128
  9.3 90.5 %all-reduce.13.cloned.1.call-start = ((), (), s32[]{:S(2)}) async-start(), calls=%async_computation.1 | async-start | bytes 524288 | tf_op jit(solution)/shard_map/psum | solution.py:211
  58.3 111.2 %all-reduce.25.cloned.1.call-start = ((), (), s32[]{:S(2)}) async-start(), calls=%async_computation.12 | async-start | bytes 1048576 | tf_op jit(solution)/shard_map/psum | solution.py:211
  58.4 111.2 %copy-start.87 = (f32[1,1,1024]{2,1,0:T(1,128)}, f32[1,1,1024]{2,1,0:T(1,128)S(1)}, u32[]{:S(2)}) copy-start(f32[1,1,1024]{2,1,0:T(1,128)S(1)} %convert_add_fusion.10) | copy-start | bytes 12292
  100.9 7.9 collective-permute-start
  109.9 89.0 %copy-start.132 = (f32[128]{0:T(128)}, f32[128]{0:T(128)S(1)}, u32[]{:S(2)}) copy-start(f32[128]{0:T(128)S(1)} %broadcast_multiply_fusion.13) | copy-start | bytes 1540
  123.6 73.9 %all-gather.14.cloned.1.call-start = ((), (), s32[]{:S(2)}) async-start(), calls=%async_computation.4 | async-start | bytes 1310720 | tf_op jit(solution)/shard_map/all_gather | solution.py:315
  129.6 152.6 %all-reduce.23.cloned.1.call-start = ((), (), s32[]{:S(2)}) async-start(), calls=%async_computation.11 | async-start | bytes 1048576 | tf_op jit(solution)/shard_map/psum | solution.py:211
  171.4 32.0 %collective-permute-start.1 = (bf16[128,1024]{1,0:T(8,128)(2,1)S(1)}, bf16[128,1024]{1,0:T(8,128)(2,1)}, u32[]{:S(2)}, u32[]{:S(2)}) collective-permute-start(bf16[128,1024]{1,0:T(8,128)(2,1)S(1)} %get-tuple-element.127), channel_id=1, source_target_pairs={{0,64},{1,65},{2,66},{3,67},{4,68},{5,69},{6,70},{7,71},{8,72},{9,... | collective-permute-start | bytes 786440 | tf_op jit(solution)/shard_map/ppermute | solution.py:18
  202.0 9.6 %collective-permute-start.4 = (bf16[128,1024]{1,0:T(8,128)(2,1)S(1)}, bf16[128,1024]{1,0:T(8,128)(2,1)S(1)}, u32[]{:S(2)}, u32[]{:S(2)}) collective-permute-start(bf16[128,1024]{1,0:T(8,128)(2,1)S(1)} %fusion.187), channel_id=1, source_target_pairs={{64,0},{65,1},{66,2},{67,3},{68,4},{69,5},{70,6},{71,7},{72,8},{73... | collective-permute-start | bytes 786440 | tf_op jit(solution)/shard_map/ppermute | solution.py:18
  213.5 100.6 %copy-start.24 = (bf16[128,1024]{1,0:T(8,128)(2,1)}, bf16[128,1024]{1,0:T(8,128)(2,1)S(1)}, u32[]{:S(2)}) copy-start(bf16[128,1024]{1,0:T(8,128)(2,1)S(1)} %get-tuple-element.85) | copy-start | bytes 786436
  240.2 70.0 %all-gather.16.cloned.1.call-start = ((), (), s32[]{:S(2)}) async-start(), calls=%async_computation.5 | async-start | bytes 1310720 | tf_op jit(solution)/shard_map/all_gather | solution.py:315
  246.4 137.4 %all-gather.18.cloned.1.call-start = ((), (), s32[]{:S(2)}) async-start(), calls=%async_computation.6 | async-start | bytes 1310720 | tf_op jit(solution)/shard_map/all_gather | solution.py:315
  284.2 39.8 %collective-permute-start.2 = (bf16[128,1024]{1,0:T(8,128)(2,1)}, bf16[128,1024]{1,0:T(8,128)(2,1)}, u32[]{:S(2)}, u32[]{:S(2)}) collective-permute-start(bf16[128,1024]{1,0:T(8,128)(2,1)} %get-tuple-element.122), channel_id=1, source_target_pairs={{0,64},{1,65},{2,66},{3,67},{4,68},{5,69},{6,70},{7,71},{8,72},{9,... | collective-permute-start | bytes 786440 | tf_op jit(solution)/shard_map/ppermute | solution.py:18
  316.3 9.6 %collective-permute-start.5 = (bf16[128,1024]{1,0:T(8,128)(2,1)S(1)}, bf16[128,1024]{1,0:T(8,128)(2,1)S(1)}, u32[]{:S(2)}, u32[]{:S(2)}) collective-permute-start(bf16[128,1024]{1,0:T(8,128)(2,1)S(1)} %get-tuple-element.95), channel_id=1, source_target_pairs={{64,0},{65,1},{66,2},{67,3},{68,4},{69,5},{70,6},{71,7},{72,8},{73... | collective-permute-start | bytes 786440 | tf_op jit(solution)/shard_map/ppermute | solution.py:18
  358.9 70.0 %all-reduce.21.cloned.1.call-start = ((), (), s32[]{:S(2)}) async-start(), calls=%async_computation.10 | async-start | bytes 1048576 | tf_op jit(solution)/shard_map/psum | solution.py:211
  374.0 130.0 %all-gather.20.cloned.1.call-start = ((), (), s32[]{:S(2)}) async-start(), calls=%async_computation.7 | async-start | bytes 1310720 | tf_op jit(solution)/shard_map/all_gather | solution.py:315
  433.4 8.6 %collective-permute-start.6 = (bf16[128,1024]{1,0:T(8,128)(2,1)S(1)}, bf16[128,1024]{1,0:T(8,128)(2,1)S(1)}, u32[]{:S(2)}, u32[]{:S(2)}) collective-permute-start(bf16[128,1024]{1,0:T(8,128)(2,1)S(1)} %get-tuple-element.93), channel_id=1, source_target_pairs={{64,0},{65,1},{66,2},{67,3},{68,4},{69,5},{70,6},{71,7},{72,8},{73... | collective-permute-start | bytes 786440 | tf_op jit(solution)/shard_map/ppermute | solution.py:18
  434.6 8.8 %collective-permute-start.3 = (bf16[128,1024]{1,0:T(8,128)(2,1)S(1)}, bf16[128,1024]{1,0:T(8,128)(2,1)S(1)}, u32[]{:S(2)}, u32[]{:S(2)}) collective-permute-start(bf16[128,1024]{1,0:T(8,128)(2,1)S(1)} %get-tuple-element.154), channel_id=1, source_target_pairs={{0,64},{1,65},{2,66},{3,67},{4,68},{5,69},{6,70},{7,71},{8,72},{9,... | collective-permute-start | bytes 786440 | tf_op jit(solution)/shard_map/ppermute | solution.py:18
  475.4 72.0 %all-reduce.15.cloned.1.call-start = ((), (), s32[]{:S(2)}) async-start(), calls=%async_computation.2 | async-start | bytes 524288 | tf_op jit(solution)/shard_map/psum | solution.py:319
  491.8 102.3 %all-gather.22.cloned.1.call-start = ((), (), s32[]{:S(2)}) async-start(), calls=%async_computation.8 | async-start | bytes 1310720 | tf_op jit(solution)/shard_map/all_gather | solution.py:315
  551.4 8.6 %collective-permute-start.7 = (bf16[128,1024]{1,0:T(8,128)(2,1)S(1)}, bf16[128,1024]{1,0:T(8,128)(2,1)S(1)}, u32[]{:S(2)}, u32[]{:S(2)}) collective-permute-start(bf16[128,1024]{1,0:T(8,128)(2,1)S(1)} %get-tuple-element.91), channel_id=1, source_target_pairs={{64,0},{65,1},{66,2},{67,3},{68,4},{69,5},{70,6},{71,7},{72,8},{73... | collective-permute-start | bytes 786440 | tf_op jit(solution)/shard_map/ppermute | solution.py:18
  564.8 70.4 %all-reduce.19.cloned.1.call-start = ((), (), s32[]{:S(2)}) async-start(), calls=%async_computation.9 | async-start | bytes 1048576 | tf_op jit(solution)/shard_map/psum | solution.py:211
  570.6 206.8 %all-reduce.17.cloned.1.call-start = ((), (), s32[]{:S(2)}) async-start(), calls=%async_computation.3 | async-start | bytes 12615680 | tf_op jit(solution)/shard_map/psum | solution.py:356
  (293 other events, 3273.1 us)
Sparse Core Ops, SparseCore 0:
  10.3 36.2 all-gather.11
  58.4 41.2 all-reduce.12
  123.7 45.7 all-reduce.24
  171.8 25.6 all-gather.13
  240.3 41.8 all-reduce.22
  284.4 25.6 all-gather.15
  359.0 24.6 all-gather.17
  386.3 42.6 all-reduce.20
  475.5 28.4 all-gather.19
  506.3 41.0 all-reduce.14
  564.9 25.3 all-gather.21
  592.6 42.6 all-reduce.18
  638.4 138.8 all-reduce.16
